TPU v7x, 32 devices: a whole 2x2x4 slice. The times are simulated.
32 devices in a mesh: row: 4 (over y, x), col: 8 (over z, core).
Axes of the slice: x: 2, y: 2, z: 4, core: 2. Of those that a mesh axis runs over, the one named last changes fastest.
Arguments:
- layer_input: float32 [2048, 1088], P('col', 'row'), may hold values from -6 to 6
- output_grad: float32 [2048, 1088], P('col', 'row'), may hold values from -6 to 6
- w_qkv: float32 [1088, 6144], P('row', 'col'), as said below
- w_out: float32 [2048, 1088], P('col', 'row'), as said below
- w_up: float32 [1088, 4352], P('row', 'col'), may hold values from -0.1875 to 0.1875
- w_down: float32 [4352, 1088], P('col', 'row'), may hold values from -0.09375 to 0.09375
- layernorm_params: float32 [4, 1088], P(None, 'row')
- state_qkv: float32 [2, 1088, 6144], P(None, 'row', 'col'), as said below
- state_out: float32 [2, 2048, 1088], P(None, 'col', 'row'), as said below
- state_up: float32 [2, 1088, 4352], P(None, 'row', 'col'), as said below
- state_down: float32 [2, 4352, 1088], P(None, 'col', 'row'), as said below
- state_norms: float32 [2, 4, 1088], P(None, None, 'row'), as said below
- segment_ids: int32 [4, 512], P('row'), may hold values from 0 to 2, as said below
Outputs:
- block_output: float32 [2048, 1088], P('col', 'row')
- layer_input_grad: float32 [2048, 1088], P('col', 'row')
- grad_qkv: float32 [1088, 6144], P('row', 'col')
- grad_out: float32 [2048, 1088], P('col', 'row')
- grad_up: float32 [1088, 4352], P('row', 'col')
- grad_down: float32 [4352, 1088], P('col', 'row')
- norm_params_grad: float32 [4, 1088], P(None, 'row')
- new_qkv: float32 [1088, 6144], P('row', 'col')
- new_out: float32 [2048, 1088], P('col', 'row')
- new_up: float32 [1088, 4352], P('row', 'col')
- new_down: float32 [4352, 1088], P('col', 'row')
- new_norms: float32 [4, 1088], P(None, 'row')
- next_state_qkv: float32 [2, 1088, 6144], P(None, 'row', 'col')
- next_state_out: float32 [2, 2048, 1088], P(None, 'col', 'row')
- next_state_up: float32 [2, 1088, 4352], P(None, 'row', 'col')
- next_state_down: float32 [2, 4352, 1088], P(None, 'col', 'row')
- next_state_norms: float32 [2, 4, 1088], P(None, None, 'row')
Inputs may be any that keep to these rules, and one draw needn't show every extreme that they name: `segment_ids`: within each sequence the ids never fall; each sequence holds exactly three documents, numbered 0, 1, 2, the first two of 64 or more tokens. `w_qkv`: columns of heads 17 and above are zero. `w_out`: rows of heads 17 and above are zero. `state_qkv`: both moments are zero in the columns of heads 17 and above; second moments are positive elsewhere. `state_out`: both moments are zero in the rows of heads 17 and above; second moments are positive elsewhere. `state_up`: second moments are positive. `state_down`: second moments are positive. `state_norms`: second moments are positive.
All inputs are finite; a program needn't handle non-finite values.
Results may differ from a plain program's by a relative error of at most 0.011.
Values may be sent and summed in bfloat16 or wider, within the bound.
No kernel may reach another device: no remote copies, remote signals or barrier semaphores. Data moves between devices by JAX's collectives and lax.ppermute only.
A program may use at most 128 MiB of HBM per device.

v0:
```python
import jax
import jax.numpy as jnp
from jax import lax
from jax.sharding import PartitionSpec as P

MODEL_WIDTH = 1088
HS = 64
SEQ = 512
EPS_NORM = 1e-05
NEG_FILL = -1e30
BETA_ONE = 0.9
BETA_TWO = 0.95
RATE = 0.01
DECAY = 0.1
STEP_COUNT = 3
ADAM_EPS = 1e-08


def row_product(left, right):
    return lax.dot_general(
        left, right, (((0,), (0,)), ((), ())), preferred_element_type=jnp.float32
    )


def back_product(left, right):
    return lax.dot_general(
        left, right, (((1,), (1,)), ((), ())), preferred_element_type=jnp.float32
    )


def layernorm_forward(x, norm_gain, shift_bias):
    total = lax.psum(jnp.sum(x, axis=1), "row")
    mean_removed = x - (total / MODEL_WIDTH)[:, None]
    spread = lax.psum(jnp.sum(mean_removed * mean_removed, axis=1), "row")
    inverse_deviation = lax.rsqrt(spread / MODEL_WIDTH + EPS_NORM)[:, None]
    normalized_rows = mean_removed * inverse_deviation
    return (
        normalized_rows,
        inverse_deviation,
        (normalized_rows * norm_gain + shift_bias).astype(jnp.bfloat16),
    )


def layernorm_backward(incoming_grad, normalized_rows, inverse_deviation, norm_gain):
    normalized_grad = incoming_grad * norm_gain
    first_branch, second_branch = lax.psum(
        (jnp.sum(normalized_grad, axis=1), jnp.sum(normalized_grad * normalized_rows, axis=1)),
        "row",
    )
    return inverse_deviation * (
        normalized_grad
        - (first_branch / MODEL_WIDTH)[:, None]
        - normalized_rows * (second_branch / MODEL_WIDTH)[:, None]
    )


def activation(value):
    return jax.nn.gelu(value, approximate=True)


def slope(value, incoming_grad):
    return jax.vjp(activation, value)[1](incoming_grad)[0]


def spread_in(acts, weight):
    gathered = lax.all_gather(acts, "col", axis=0, tiled=True)
    widened = lax.all_to_all(gathered, "row", split_axis=0, concat_axis=1, tiled=True)
    whole = lax.all_gather(weight, "row", axis=0, tiled=True)
    return ((widened, whole), jnp.dot(widened, whole, preferred_element_type=jnp.float32))


def spread_out(branch, weight):
    gathered = lax.all_gather(branch, "row", axis=0, tiled=True)
    return (
        gathered,
        lax.psum_scatter(
            jnp.dot(gathered, weight, preferred_element_type=jnp.float32),
            "col",
            scatter_dimension=0,
            tiled=True,
        ),
    )


def back_in(grad, kept):
    widened, whole = kept
    weight_grad = lax.psum_scatter(
        row_product(widened, grad), "row", scatter_dimension=0, tiled=True
    )
    partial_value = back_product(grad, whole)
    moved = lax.all_to_all(partial_value, "row", split_axis=1, concat_axis=0, tiled=True)
    return (weight_grad, lax.psum_scatter(moved, "col", scatter_dimension=0, tiled=True))


def back_out(grad, gathered, weight):
    full = lax.all_gather(grad, "col", axis=0, tiled=True)
    weight_grad = row_product(gathered, full)
    return (
        weight_grad,
        lax.psum_scatter(back_product(full, weight), "row", scatter_dimension=0, tiled=True),
    )


def masked_scores(query, keys, segment):
    scores = jnp.einsum("qhd,khd->hqk", query, keys, preferred_element_type=jnp.float32) * HS ** (
        -0.5
    )
    place = jnp.arange(segment.shape[0])
    allowed = (place[None, :] <= place[:, None]) & (segment[None, :] == segment[:, None])
    return jnp.where(allowed[None], scores, NEG_FILL)


def attend(item):
    block, segment = item
    query, keys, values = (block[:, :, 0], block[:, :, 1], block[:, :, 2])
    scores = masked_scores(query, keys, segment)
    top = jnp.max(scores, axis=-1)
    lse = top + jnp.log(jnp.sum(jnp.exp(scores - top[..., None]), axis=-1))
    probs = jnp.exp(scores - lse[..., None]).astype(jnp.bfloat16)
    result = jnp.einsum("hqk,khd->qhd", probs, values, preferred_element_type=jnp.float32)
    return (result.astype(jnp.bfloat16), lse)


def attend_back(item):
    block, segment, lse, incoming_grad = item
    query, keys, values = (block[:, :, 0], block[:, :, 1], block[:, :, 2])
    probs = jnp.exp(masked_scores(query, keys, segment) - lse[..., None])
    probs_low = probs.astype(jnp.bfloat16)
    dvalues = jnp.einsum(
        "hqk,qhd->khd", probs_low, incoming_grad, preferred_element_type=jnp.float32
    )
    dprobs = jnp.einsum("qhd,khd->hqk", incoming_grad, values, preferred_element_type=jnp.float32)
    delta = jnp.sum(probs * dprobs, axis=-1, keepdims=True)
    dscores = (probs * (dprobs - delta)).astype(jnp.bfloat16)
    dquery = jnp.einsum("hqk,khd->qhd", dscores, keys, preferred_element_type=jnp.float32) * HS ** (
        -0.5
    )
    dkeys = jnp.einsum("hqk,qhd->khd", dscores, query, preferred_element_type=jnp.float32) * HS ** (
        -0.5
    )
    return jnp.stack([dquery, dkeys, dvalues], axis=2).astype(jnp.bfloat16)


def adamw(param, grad, state, decay):
    first_branch = BETA_ONE * state[0] + (1.0 - BETA_ONE) * grad
    second_branch = BETA_TWO * state[1] + (1.0 - BETA_TWO) * grad * grad
    first_hat = first_branch / (1.0 - BETA_ONE**STEP_COUNT)
    second_hat = second_branch / (1.0 - BETA_TWO**STEP_COUNT)
    updated = param - RATE * (first_hat / (jnp.sqrt(second_hat) + ADAM_EPS) + decay * param)
    return (updated, jnp.stack([first_branch, second_branch]))


def shards(
    layer_input,
    output_grad,
    w_qkv,
    w_out,
    w_up,
    w_down,
    layernorm_params,
    state_qkv,
    state_out,
    state_up,
    state_down,
    state_norms,
    segment_ids,
):
    low = jnp.bfloat16
    wq, wo, wu, wd = (w_qkv.astype(low), w_out.astype(low), w_up.astype(low), w_down.astype(low))
    local_seqs = segment_ids.shape[0]
    normalized_rows1, inverse_deviation1, attention_input = layernorm_forward(
        layer_input, layernorm_params[0], layernorm_params[1]
    )
    kept_first, qkv_sum = spread_in(attention_input, wq)
    blocks = qkv_sum.astype(low).reshape(local_seqs, SEQ, -1, 3, HS)
    attended, lse = lax.map(attend, (blocks, segment_ids))
    attended = attended.reshape(local_seqs * SEQ, -1)
    kept_attended, attn_sum = spread_out(attended, wo)
    middle_stream = layer_input + attn_sum
    normalized_rows2, inverse_deviation2, feedforward_input = layernorm_forward(
        middle_stream, layernorm_params[2], layernorm_params[3]
    )
    kept_second, pre = spread_in(feedforward_input, wu)
    hidden = activation(pre).astype(low)
    kept_hidden, mlp_sum = spread_out(hidden, wd)
    block_output = middle_stream + mlp_sum
    out_low = output_grad.astype(low)
    grad_down, hidden_grad = back_out(out_low, kept_hidden, wd)
    pre_grad = slope(pre, hidden_grad).astype(low)
    grad_up, feedforward_input_grad = back_in(pre_grad, kept_second)
    middle_stream_grad = output_grad + layernorm_backward(
        feedforward_input_grad, normalized_rows2, inverse_deviation2, layernorm_params[2]
    )
    middle_low = middle_stream_grad.astype(low)
    grad_out, attended_grad = back_out(middle_low, kept_attended, wo)
    incoming_grad = attended_grad.astype(low).reshape(local_seqs, SEQ, -1, HS)
    qkv_grad = lax.map(attend_back, (blocks, segment_ids, lse, incoming_grad)).reshape(
        local_seqs * SEQ, -1
    )
    grad_qkv, attention_input_grad = back_in(qkv_grad, kept_first)
    layer_input_grad = middle_stream_grad + layernorm_backward(
        attention_input_grad, normalized_rows1, inverse_deviation1, layernorm_params[0]
    )
    local_terms = jnp.stack(
        [
            jnp.sum(attention_input_grad * normalized_rows1, axis=0),
            jnp.sum(attention_input_grad, axis=0),
            jnp.sum(feedforward_input_grad * normalized_rows2, axis=0),
            jnp.sum(feedforward_input_grad, axis=0),
        ]
    )
    norm_params_grad = lax.psum(local_terms, "col")
    new_qkv, next_state_qkv = adamw(w_qkv, grad_qkv, state_qkv, DECAY)
    new_out, next_state_out = adamw(w_out, grad_out, state_out, DECAY)
    new_up, next_state_up = adamw(w_up, grad_up, state_up, DECAY)
    new_down, next_state_down = adamw(w_down, grad_down, state_down, DECAY)
    new_norms, next_state_norms = adamw(layernorm_params, norm_params_grad, state_norms, 0.0)
    return (
        block_output,
        layer_input_grad,
        grad_qkv,
        grad_out,
        grad_up,
        grad_down,
        norm_params_grad,
        new_qkv,
        new_out,
        new_up,
        new_down,
        new_norms,
        next_state_qkv,
        next_state_out,
        next_state_up,
        next_state_down,
        next_state_norms,
    )


def solution(mesh):
    placed = (
        P("col", "row"),
        P("col", "row"),
        P("row", "col"),
        P("col", "row"),
        P("row", "col"),
        P("col", "row"),
        P(None, "row"),
        P(None, "row", "col"),
        P(None, "col", "row"),
        P(None, "row", "col"),
        P(None, "col", "row"),
        P(None, None, "row"),
        P("row", None),
    )
    return jax.shard_map(
        shards,
        mesh=mesh,
        in_specs=placed,
        out_specs=(
            P("col", "row"),
            P("col", "row"),
            P("row", "col"),
            P("col", "row"),
            P("row", "col"),
            P("col", "row"),
            P(None, "row"),
            P("row", "col"),
            P("col", "row"),
            P("row", "col"),
            P("col", "row"),
            P(None, "row"),
            P(None, "row", "col"),
            P(None, "col", "row"),
            P(None, "row", "col"),
            P(None, "col", "row"),
            P(None, None, "row"),
        ),
        check_vma=False,
    )
```

profile of v0, /device:TPU:0, one launch (start us, length us, event | category | flops | bytes accessed | tf_op | source)
XLA Modules:
  0.0 672.1 jit_solution(4915500629032504406)
XLA Ops:
  7.2 1.1 reduce_sum.128
  8.3 11.4 %psum.63 = f32[256]{0:T(256)S(1)} all-reduce(f32[256]{0:T(256)S(1)} %reduce_sum.128), channel_id=1, replica_groups=mesh['row'=4,'col'=8] {'row'}, use_global_device_ids=true, to_apply=%region_1.0 | all-reduce | flops 256 | bytes 2048 | tf_op jit(solution)/shard_map/psum | solution.py:32
  19.7 1.0 multiply_reduce_fusion.6
  20.7 8.0 %psum.64 = f32[256]{0:T(256)S(1)} all-reduce(f32[256]{0:T(256)S(1)} %multiply_reduce_fusion.6), channel_id=1, replica_groups=mesh['row'=4,'col'=8] {'row'}, use_global_device_ids=true, to_apply=%region_3.0 | all-reduce | flops 256 | bytes 2048 | tf_op jit(solution)/shard_map/psum | solution.py:34
  29.6 1.8 add_convert_fusion.1
  32.2 23.8 %all-gather.9.cloned.1.call-done = bf16[2048,272]{0,1:T(8,128)(2,1)} async-done(((bf16[256,272]{0,1:T(8,128)(2,1)}), bf16[2048,272]{0,1:T(8,128)(2,1)}) %all-gather.9.cloned.1.call-update) | async-done | bytes 1114128 | tf_op jit(solution)/shard_map/all_gather | solution.py:66
  56.1 2.3 copy.87
  58.4 3.7 all-to-all-start
  62.3 35.0 %all-gather.11.cloned.1.call-done = bf16[1088,768]{1,0:T(8,128)(2,1)} async-done(((bf16[272,768]{1,0:T(8,128)(2,1)}), bf16[1088,768]{1,0:T(8,128)(2,1)}) %all-gather.11.cloned.1.call-update) | async-done | bytes 1671184 | tf_op jit(solution)/shard_map/all_gather | solution.py:68
  97.3 3.6 convolution_convert_fusion
  100.9 1.4 copy.57
  105.2 2.0 convolution_convert_fusion.2
  107.2 26.5 %all-gather.13.cloned.1.call-done = bf16[2048,256]{0,1:T(8,128)(2,1)} async-done(((bf16[512,256]{0,1:T(8,128)(2,1)}), bf16[2048,256]{0,1:T(8,128)(2,1)}) %all-gather.13.cloned.1.call-update) | async-done | bytes 1048592 | tf_op jit(solution)/shard_map/all_gather | solution.py:73
  133.7 3.1 fusion.34
  138.5 34.9 %reduce-scatter.11.cloned.1.call-done = f32[256,272]{0,1:T(8,128)} async-done(((f32[2048,272]{0,1:T(8,128)}), f32[256,272]{0,1:T(8,128)}) %reduce-scatter.11.cloned.1.call-update) | async-done | bytes 278544 | tf_op jit(solution)/shard_map/reduce_scatter | solution.py:76
  173.4 1.0 fusion.43
  174.4 9.8 %psum.65 = f32[256]{0:T(256)S(1)} all-reduce(f32[256]{0:T(256)S(1)} %get-tuple-element.68), channel_id=1, replica_groups=mesh['row'=4,'col'=8] {'row'}, use_global_device_ids=true, to_apply=%region_8.9 | all-reduce | flops 256 | bytes 2048 | tf_op jit(solution)/shard_map/psum | solution.py:32
  184.4 8.2 %psum.66 = f32[256]{0:T(256)S(1)} all-reduce(f32[256]{0:T(256)S(1)} %multiply_reduce_fusion.5), channel_id=1, replica_groups=mesh['row'=4,'col'=8] {'row'}, use_global_device_ids=true, to_apply=%region_10.11 | all-reduce | flops 256 | bytes 2048 | tf_op jit(solution)/shard_map/psum | solution.py:34
  194.3 4.3 all-gather.21.cloned.1.call-done
  198.6 4.7 fusion.24
  203.4 20.2 %all-gather.15.cloned.1.call-done = bf16[2048,272]{0,1:T(8,128)(2,1)} async-done(((bf16[256,272]{0,1:T(8,128)(2,1)}), bf16[2048,272]{0,1:T(8,128)(2,1)}) %all-gather.15.cloned.1.call-update) | async-done | bytes 1114128 | tf_op jit(solution)/shard_map/all_gather | solution.py:66
  223.6 2.3 copy.86
  225.9 3.5 all-to-all-start.1
  229.5 33.0 %all-gather.17.cloned.1.call-done = bf16[1088,544]{1,0:T(8,128)(2,1)} async-done(((bf16[272,544]{1,0:T(8,128)(2,1)}), bf16[1088,544]{1,0:T(8,128)(2,1)}) %all-gather.17.cloned.1.call-update) | async-done | bytes 1183760 | tf_op jit(solution)/shard_map/all_gather | solution.py:68
  262.5 57.9 %reduce-scatter.15.cloned.1.call-done = f32[512,544]{0,1:T(8,128)} async-done(((f32[2048,544]{0,1:T(8,128)}), f32[512,544]{0,1:T(8,128)}) %reduce-scatter.15.cloned.1.call-update) | async-done | bytes 1114128 | tf_op jit(solution)/shard_map/reduce_scatter | solution.py:100
  320.4 4.3 fusion.13
  324.7 2.5 fusion.49
  327.2 36.8 %all_to_all.73 = f32[512,4,272]{0,2,1:T(8,128)S(1)} all-to-all(f32[512,4,272]{0,2,1:T(8,128)S(1)} %bitcast.188), channel_id=1, replica_groups=mesh['row'=4,'col'=8] {'row'}, dimensions={1} | all-to-all | bytes 4456448 | tf_op jit(solution)/shard_map/all_to_all | solution.py:91
  364.0 1.6 copy.82
  365.7 8.5 %all-gather.19.cloned.1.call-done = bf16[2048,544]{0,1:T(8,128)(2,1)} async-done(((bf16[512,544]{0,1:T(8,128)(2,1)}), bf16[2048,544]{0,1:T(8,128)(2,1)}) %all-gather.19.cloned.1.call-update) | async-done | bytes 2228240 | tf_op jit(solution)/shard_map/all_gather | solution.py:73
  374.2 4.0 fusion.26
  378.3 34.5 %reduce-scatter.17.cloned.1.call-done = f32[256,272]{0,1:T(8,128)} async-done(((f32[2048,272]{0,1:T(8,128)}), f32[256,272]{0,1:T(8,128)}) %reduce-scatter.17.cloned.1.call-update) | async-done | bytes 278544 | tf_op jit(solution)/shard_map/reduce_scatter | solution.py:92
  412.8 1.2 multiply_reduce_fusion.1
  414.0 10.2 %all-reduce.2 = (f32[256]{0:T(256)S(1)}, f32[256]{0:T(256)S(1)}) all-reduce(f32[256]{0:T(256)S(1)} %get-tuple-element.53, f32[256]{0:T(256)S(1)} %get-tuple-element.54), channel_id=1, replica_groups=mesh['row'=4,'col'=8] {'row'}, use_global_device_ids=true, to_apply=%region_17.18 | all-reduce | flops 512 | bytes 4096 | tf_op jit(solution)/shard_map/psum | solution.py:46
  424.2 26.2 %reduce-scatter.13.cloned.1.call-done = f32[256,272]{0,1:T(8,128)} async-done(((f32[2048,272]{0,1:T(8,128)}), f32[256,272]{0,1:T(8,128)}) %reduce-scatter.13.cloned.1.call-update) | async-done | bytes 278544 | tf_op jit(solution)/shard_map/reduce_scatter | solution.py:76
  450.4 2.1 fusion.42
  452.6 23.1 %all-gather.23.cloned.1.call-done = bf16[2048,272]{0,1:T(8,128)(2,1)} async-done(((bf16[256,272]{0,1:T(8,128)(2,1)}), bf16[2048,272]{0,1:T(8,128)(2,1)}) %all-gather.23.cloned.1.call-update) | async-done | bytes 1114128 | tf_op jit(solution)/shard_map/all_gather | solution.py:96
  475.7 3.4 fusion.32
  479.2 3.8 fusion.47
  483.0 30.2 %reduce-scatter.19.cloned.1.call-done = f32[512,256]{1,0:T(8,128)} async-done(((f32[2048,256]{1,0:T(8,128)}), f32[512,256]{1,0:T(8,128)}) %reduce-scatter.19.cloned.1.call-update) | async-done | bytes 524304 | tf_op jit(solution)/shard_map/reduce_scatter | solution.py:100
  513.2 1.8 convert_element_type.83
  515.0 1.1 copy.64
  516.1 3.9 multiply_reduce_fusion
  520.0 1.3 multiply_convert_fusion
  522.5 1.3 fusion.6
  523.9 1.3 copy-done.28
  525.2 1.0 fusion.44
  526.2 38.4 %all_to_all.74 = f32[512,4,272]{0,2,1:T(8,128)S(1)} all-to-all(f32[512,4,272]{0,2,1:T(8,128)S(1)} %fusion.44), channel_id=1, replica_groups=mesh['row'=4,'col'=8] {'row'}, dimensions={1} | all-to-all | bytes 4456448 | tf_op jit(solution)/shard_map/all_to_all | solution.py:91
  564.6 1.6 copy.83
  566.2 2.8 fusion.45
  569.0 1.2 copy-done.14
  570.3 2.9 fusion.48
  573.2 1.4 fusion.23
  574.6 1.2 pad_maximum_fusion.2
  576.6 2.5 fusion.22
  579.1 1.2 pad_maximum_fusion.1
  583.5 29.9 %reduce-scatter.21.cloned.1.call-done = f32[256,272]{0,1:T(8,128)} async-done(((f32[2048,272]{0,1:T(8,128)}), f32[256,272]{0,1:T(8,128)}) %reduce-scatter.21.cloned.1.call-update) | async-done | bytes 278544 | tf_op jit(solution)/shard_map/reduce_scatter | solution.py:92
  613.4 1.2 multiply_reduce_fusion.2
  614.6 9.8 %all-reduce.1 = (f32[256]{0:T(256)S(1)}, f32[256]{0:T(256)S(1)}) all-reduce(f32[256]{0:T(256)S(1)} %get-tuple-element.51, f32[256]{0:T(256)S(1)} %get-tuple-element.55), channel_id=1, replica_groups=mesh['row'=4,'col'=8] {'row'}, use_global_device_ids=true, to_apply=%region_24.25 | all-reduce | flops 512 | bytes 4096 | tf_op jit(solution)/shard_map/psum | solution.py:46
  624.5 13.9 %psum.71 = f32[4,272]{1,0:T(4,128)S(1)} all-reduce(f32[4,272]{1,0:T(4,128)S(1)} %pad_maximum_fusion.6), channel_id=1, replica_groups=mesh['row'=4,'col'=8] {'col'}, use_global_device_ids=true, to_apply=%region_31.32 | all-reduce | flops 1088 | bytes 8704 | tf_op jit(solution)/shard_map/psum | solution.py:212
  639.6 1.8 multiply_add_fusion
  641.4 19.7 %reduce-scatter.23.cloned.1.call-done = f32[272,768]{1,0:T(8,128)} async-done(((f32[1088,768]{1,0:T(8,128)}), f32[272,768]{1,0:T(8,128)}) %reduce-scatter.23.cloned.1.call-update) | async-done | bytes 835600 | tf_op jit(solution)/shard_map/reduce_scatter | solution.py:87
  661.1 3.2 fusion.21
  664.3 1.3 pad_maximum_fusion
  (122 shorter events, 15.6 us)
Async XLA Ops:
  7.2 24.2 %copy-start.10 = (f32[272,768]{1,0:T(8,128)S(1)}, f32[272,768]{1,0:T(8,128)}, u32[]{:S(2)}) copy-start(f32[272,768]{1,0:T(8,128)} %param.15) | copy-start | bytes 2506756
  7.2 48.9 %all-gather.9.cloned.1.call-start = ((), (), s32[]{:S(2)}) async-start(), calls=%async_computation.12 | async-start | bytes 1253376 | tf_op jit(solution)/shard_map/all_gather | solution.py:66
  31.4 66.0 %all-gather.11.cloned.1.call-start = ((), (), s32[]{:S(2)}) async-start(), calls=%async_computation.13 | async-start | bytes 2088960 | tf_op jit(solution)/shard_map/all_gather | solution.py:68
  58.4 3.7 copy-start.27
  58.4 38.9 %all-to-all-start = ((bf16[4,512,272]{1,2,0:T(8,128)(2,1)}), bf16[4,512,272]{1,2,0:T(8,128)(2,1)S(1)}, u32[]{:S(2)}, u32[]{:S(2)}) async-start(bf16[4,512,272]{1,2,0:T(8,128)(2,1)} %bitcast.171), calls=%async_computation | async-start | bytes 2228224 | tf_op jit(solution)/shard_map/all_to_all | solution.py:67
  62.1 71.7 %all-gather.13.cloned.1.call-start = ((), (), s32[]{:S(2)}) async-start(), calls=%async_computation.14 | async-start | bytes 1310720 | tf_op jit(solution)/shard_map/all_gather | solution.py:73
  62.3 41.9 %copy-start.8 = (pred[512,512]{0,1:T(8,128)(4,1)}, pred[512,512]{0,1:T(8,128)(4,1)S(1)}, u32[]{:S(2)}) copy-start(pred[512,512]{0,1:T(8,128)(4,1)S(1)} %fusion.14) | copy-start | bytes 786436
  102.3 1.9 copy-start.12
  103.2 2.0 copy-start
  105.2 28.5 %copy-start.5 = (f32[256,272]{0,1:T(8,128)S(1)}, f32[256,272]{0,1:T(8,128)}, u32[]{:S(2)}) copy-start(f32[256,272]{0,1:T(8,128)} %param.16) | copy-start | bytes 835588
  107.2 66.2 %reduce-scatter.11.cloned.1.call-start = ((), (), s32[]{:S(2)}) async-start(), calls=%async_computation.15 | async-start | bytes 2506752 | tf_op jit(solution)/shard_map/reduce_scatter | solution.py:76
  136.8 1.0 copy-start.19
  136.8 36.6 %copy-start.2 = (f32[256,272]{0,1:T(8,128)S(1)}, f32[256,272]{0,1:T(8,128)}, u32[]{:S(2)}) copy-start(f32[256,272]{0,1:T(8,128)} %param.13) | copy-start | bytes 835588
  136.9 56.6 %copy-start.15 = (f32[272,544]{1,0:T(8,128)S(1)}, f32[272,544]{1,0:T(8,128)}, u32[]{:S(2)}) copy-start(f32[272,544]{1,0:T(8,128)} %param.17) | copy-start | bytes 1775620
  136.9 61.7 %all-gather.21.cloned.1.call-start = ((), (), s32[]{:S(2)}) async-start(), calls=%async_computation.20 | async-start | bytes 1253376 | tf_op jit(solution)/shard_map/all_gather | solution.py:96
  138.5 60.1 %copy-start.3 = (f32[544,272]{0,1:T(8,128)S(1)}, f32[544,272]{0,1:T(8,128)}, u32[]{:S(2)}) copy-start(f32[544,272]{0,1:T(8,128)} %param.18) | copy-start | bytes 1775620
  138.5 85.1 %all-gather.15.cloned.1.call-start = ((), (), s32[]{:S(2)}) async-start(), calls=%async_computation.16 | async-start | bytes 1253376 | tf_op jit(solution)/shard_map/all_gather | solution.py:66
  193.4 69.1 %all-gather.17.cloned.1.call-start = ((), (), s32[]{:S(2)}) async-start(), calls=%async_computation.17 | async-start | bytes 1740800 | tf_op jit(solution)/shard_map/all_gather | solution.py:68
  194.2 126.1 %reduce-scatter.15.cloned.1.call-start = ((), (), s32[]{:S(2)}) async-start(), calls=%async_computation.21 | async-start | bytes 5570560 | tf_op jit(solution)/shard_map/reduce_scatter | solution.py:100
  225.9 94.4 %all-to-all-start.1 = ((bf16[4,512,272]{1,2,0:T(8,128)(2,1)}), bf16[4,512,272]{1,2,0:T(8,128)(2,1)S(1)}, u32[]{:S(2)}, u32[]{:S(2)}) async-start(bf16[4,512,272]{1,2,0:T(8,128)(2,1)} %bitcast.180), calls=%async_computation.2 | async-start | bytes 2228224 | tf_op jit(solution)/shard_map/all_to_all | solution.py:67
  229.5 144.7 %all-gather.19.cloned.1.call-start = ((), (), s32[]{:S(2)}) async-start(), calls=%async_computation.18 | async-start | bytes 2785280 | tf_op jit(solution)/shard_map/all_gather | solution.py:73
  324.7 88.1 %reduce-scatter.17.cloned.1.call-start = ((), (), s32[]{:S(2)}) async-start(), calls=%async_computation.22 | async-start | bytes 2506752 | tf_op jit(solution)/shard_map/reduce_scatter | solution.py:92
  365.7 84.7 %reduce-scatter.13.cloned.1.call-start = ((), (), s32[]{:S(2)}) async-start(), calls=%async_computation.19 | async-start | bytes 2506752 | tf_op jit(solution)/shard_map/reduce_scatter | solution.py:76
  378.2 97.5 %all-gather.23.cloned.1.call-start = ((), (), s32[]{:S(2)}) async-start(), calls=%async_computation.23 | async-start | bytes 1253376 | tf_op jit(solution)/shard_map/all_gather | solution.py:96
  452.5 60.6 %reduce-scatter.19.cloned.1.call-start = ((), (), s32[]{:S(2)}) async-start(), calls=%async_computation.24 | async-start | bytes 2621440 | tf_op jit(solution)/shard_map/reduce_scatter | solution.py:100
  479.1 96.6 %reduce-scatter.25.cloned.1.call-start = ((), (), s32[]{:S(2)}) async-start(), calls=%async_computation.27 | async-start | bytes 3481600
  482.9 33.1 %copy-start.9 = (pred[512,512]{0,1:T(8,128)(4,1)S(1)}, pred[512,512]{0,1:T(8,128)(4,1)}, u32[]{:S(2)}) copy-start(pred[512,512]{0,1:T(8,128)(4,1)} %copy-done.8) | copy-start | bytes 786436
  482.9 33.1 %copy-start.13 = (bf16[512,768]{0,1:T(8,128)(2,1)S(1)}, bf16[512,768]{0,1:T(8,128)(2,1)}, u32[]{:S(2)}) copy-start(bf16[512,768]{0,1:T(8,128)(2,1)} %copy-done.12) | copy-start | bytes 2359300
  483.0 130.4 %reduce-scatter.21.cloned.1.call-start = ((), (), s32[]{:S(2)}) async-start(), calls=%async_computation.25 | async-start | bytes 2506752 | tf_op jit(solution)/shard_map/reduce_scatter | solution.py:92
  516.1 3.9 copy-start.1
  523.7 1.4 copy-start.28
  566.2 94.9 %reduce-scatter.23.cloned.1.call-start = ((), (), s32[]{:S(2)}) async-start(), calls=%async_computation.26 | async-start | bytes 4177920 | tf_op jit(solution)/shard_map/reduce_scatter | solution.py:87
  569.0 1.3 copy-start.14
  570.3 2.9 copy-start.17
  573.1 1.4 copy-start.22
  574.5 1.3 copy-start.16
  574.6 2.1 copy-start.18
  579.1 1.8 copy-start.4
  579.1 2.1 copy-start.7
  580.3 1.4 copy-start.6
  580.3 1.4 copy-start.23
  581.7 32.9 %copy-start.21 = (f32[256,272]{0,1:T(8,128)}, f32[256,272]{0,1:T(8,128)S(1)}, u32[]{:S(2)}) copy-start(f32[256,272]{0,1:T(8,128)S(1)} %fusion.46) | copy-start | bytes 835588
  581.7 56.7 %copy-start.24 = (f32[4,272]{1,0:T(4,128)S(1)}, f32[4,272]{1,0:T(4,128)}, u32[]{:S(2)}) copy-start(f32[4,272]{1,0:T(4,128)} %param.19) | copy-start | bytes 13060
  581.7 56.7 %copy-start.26 = (f32[2,4,272]{2,1,0:T(4,128)S(1)}, f32[2,4,272]{2,1,0:T(4,128)}, u32[]{:S(2)}) copy-start(f32[2,4,272]{2,1,0:T(4,128)} %param.24) | copy-start | bytes 26116
  581.7 57.9 %copy-start.20 = (f32[256,272]{0,1:T(8,128)S(1)}, f32[256,272]{0,1:T(8,128)}, u32[]{:S(2)}) copy-start(f32[256,272]{0,1:T(8,128)} %get-tuple-element.67) | copy-start | bytes 835588
  582.7 78.4 %copy-start.11 = (f32[272,768]{1,0:T(8,128)S(1)}, f32[272,768]{1,0:T(8,128)}, u32[]{:S(2)}) copy-start(f32[272,768]{1,0:T(8,128)} %param.15) | copy-start | bytes 2506756
  638.4 25.9 %copy-start.25 = (f32[4,272]{1,0:T(4,128)}, f32[4,272]{1,0:T(4,128)S(1)}, u32[]{:S(2)}) copy-start(f32[4,272]{1,0:T(4,128)S(1)} %psum.71) | copy-start | bytes 13060
Sparse Core Ops, SparseCore 0:
  31.5 24.5 all-gather.8
  58.5 38.8 all-gather.10
  107.3 26.3 all-gather.12
  137.0 36.3 reduce-scatter.10
  175.4 23.1 all-gather.20
  200.6 22.9 all-gather.14
  226.0 36.4 all-gather.16
  265.6 54.7 reduce-scatter.14
  324.8 49.3 all-gather.18
  376.3 36.4 reduce-scatter.16
  415.1 35.2 reduce-scatter.12
  452.7 23.0 all-gather.22
  479.3 33.8 reduce-scatter.18
  516.6 57.8 reduce-scatter.24
  576.7 36.6 reduce-scatter.20
  616.9 44.1 reduce-scatter.22
where the time goes:
time: 674 us; the launch traced here: 672 us
  waiting for transfers between devices  408 us (61%)
  blocking collectives  146 us (22%)
  matrix products  45.7 us (7%)
  other arithmetic  32.3 us (5%)
  local copies, waits for them, and re-layouts  17.5 us (3%)
  between operations  14.4 us (2%)
  starting transfers between devices  7.85 us (1%)
    reduce_scatter x2, waiting for transfers between devices, back_out(): lax.psum_scatter(back_product(full, weight), 'row', scatter_dimension=0,...  88 us
    all_to_all x2, blocking collectives, back_in(): lax.all_to_all(partial_value, 'row', split_axis=1, concat_axis=0, tiled=T...  75.2 us
    all_gather x2, waiting for transfers between devices, spread_in(): whole = lax.all_gather(weight, 'row', axis=0, tiled=True)  68 us
    reduce_scatter x2, waiting for transfers between devices, back_in(): lax.psum_scatter(moved, 'col', scatter_dimension=0, tiled=True)  64.4 us
    reduce_scatter x2, waiting for transfers between devices, spread_out(): lax.psum_scatter(jnp.dot(gathered, weight, preferred_element_type=jnp.flo...  61.1 us
    all_gather x2, waiting for transfers between devices, spread_in(): gathered = lax.all_gather(acts, 'col', axis=0, tiled=True)  44.1 us
    all_gather x2, waiting for transfers between devices, spread_out(): gathered = lax.all_gather(branch, 'row', axis=0, tiled=True)  34.9 us
    all_gather x2, waiting for transfers between devices, back_out(): full = lax.all_gather(grad, 'col', axis=0, tiled=True)  27.5 us
  transfers between devices with their start and end apart: 18, of which 15 were waited for; matrix products, arithmetic and copies ran while one was open for 9% of the time, Pallas kernels for 0%

commit v1 on v0

--- a/solution.py
+++ b/solution.py
@@ -2,6 +2,7 @@
 import jax.numpy as jnp
 from jax import lax
 from jax.sharding import PartitionSpec as P
+from jax.lax import all_to_all, axis_size
 
 MODEL_WIDTH = 1088
 HS = 64
@@ -88,7 +89,11 @@
         row_product(widened, grad), "row", scatter_dimension=0, tiled=True
     )
     partial_value = back_product(grad, whole)
-    moved = lax.all_to_all(partial_value, "row", split_axis=1, concat_axis=0, tiled=True)
+    t1 = axis_size("row")
+    mat_out = jnp.split(partial_value, t1, axis=1)
+    frame_out = jnp.stack(mat_out, axis=0)
+    formed = all_to_all(frame_out, "row", 0, 0)
+    moved = jnp.concatenate(formed, axis=0)
     return (weight_grad, lax.psum_scatter(moved, "col", scatter_dimension=0, tiled=True))
 
 

time: 674 us -> 671 us (level)
  no operation moved by 1% of the time
where the time goes in v1:
time: 671 us; the launch traced here: 669 us
  waiting for transfers between devices  405 us (60%)
  blocking collectives  146 us (22%)
  matrix products  44.7 us (7%)
  other arithmetic  33.3 us (5%)
  local copies, waits for them, and re-layouts  16.8 us (3%)
  between operations  14.4 us (2%)
  starting transfers between devices  8.11 us (1%)
    reduce_scatter x2, waiting for transfers between devices, back_out(): lax.psum_scatter(back_product(full, weight), 'row', scatter_dimension=0,...  88 us
    all_to_all x2, blocking collectives, back_in(): formed = all_to_all(frame_out, 'row', 0, 0)  75.6 us
    all_gather x2, waiting for transfers between devices, spread_in(): whole = lax.all_gather(weight, 'row', axis=0, tiled=True)  68 us
    reduce_scatter x2, waiting for transfers between devices, back_in(): lax.psum_scatter(moved, 'col', scatter_dimension=0, tiled=True)  63.5 us
    reduce_scatter x2, waiting for transfers between devices, spread_out(): lax.psum_scatter(jnp.dot(gathered, weight, preferred_element_type=jnp.flo...  61.5 us
    all_gather x2, waiting for transfers between devices, spread_in(): gathered = lax.all_gather(acts, 'col', axis=0, tiled=True)  42.9 us
    all_gather x2, waiting for transfers between devices, spread_out(): gathered = lax.all_gather(branch, 'row', axis=0, tiled=True)  33.9 us
    all_gather x2, waiting for transfers between devices, back_out(): full = lax.all_gather(grad, 'col', axis=0, tiled=True)  27.4 us
  transfers between devices with their start and end apart: 18, of which 15 were waited for; matrix products, arithmetic and copies ran while one was open for 9% of the time, Pallas kernels for 0%

profile of v1, /device:TPU:0, one launch (start us, length us, event | category | flops | bytes accessed | tf_op | source)
XLA Modules:
  0.0 669.1 jit_solution(5201548182185149208)
XLA Ops:
  7.2 1.0 reduce_sum.128
  8.2 11.4 %psum.63 = f32[256]{0:T(256)S(1)} all-reduce(f32[256]{0:T(256)S(1)} %reduce_sum.128), channel_id=1, replica_groups=mesh['row'=4,'col'=8] {'row'}, use_global_device_ids=true, to_apply=%region_1.0 | all-reduce | flops 256 | bytes 2048 | tf_op jit(solution)/shard_map/psum | solution.py:33
  19.6 1.0 multiply_reduce_fusion.6
  20.6 8.0 %psum.64 = f32[256]{0:T(256)S(1)} all-reduce(f32[256]{0:T(256)S(1)} %multiply_reduce_fusion.6), channel_id=1, replica_groups=mesh['row'=4,'col'=8] {'row'}, use_global_device_ids=true, to_apply=%region_3.0 | all-reduce | flops 256 | bytes 2048 | tf_op jit(solution)/shard_map/psum | solution.py:35
  29.5 1.8 add_convert_fusion.1
  31.3 1.9 convert_element_type.69
  33.3 22.7 %all-gather.9.cloned.1.call-done = bf16[2048,272]{0,1:T(8,128)(2,1)} async-done(((bf16[256,272]{0,1:T(8,128)(2,1)}), bf16[2048,272]{0,1:T(8,128)(2,1)}) %all-gather.9.cloned.1.call-update) | async-done | bytes 1114128 | tf_op jit(solution)/shard_map/all_gather | solution.py:67
  56.0 2.3 copy.83
  58.3 3.5 all-to-all-start
  62.1 35.0 %all-gather.11.cloned.1.call-done = bf16[1088,768]{1,0:T(8,128)(2,1)} async-done(((bf16[272,768]{1,0:T(8,128)(2,1)}), bf16[1088,768]{1,0:T(8,128)(2,1)}) %all-gather.11.cloned.1.call-update) | async-done | bytes 1671184 | tf_op jit(solution)/shard_map/all_gather | solution.py:69
  97.1 2.7 convolution_convert_fusion
  103.0 2.0 convolution_convert_fusion.1
  105.0 26.5 %all-gather.13.cloned.1.call-done = bf16[2048,256]{0,1:T(8,128)(2,1)} async-done(((bf16[512,256]{0,1:T(8,128)(2,1)}), bf16[2048,256]{0,1:T(8,128)(2,1)}) %all-gather.13.cloned.1.call-update) | async-done | bytes 1048592 | tf_op jit(solution)/shard_map/all_gather | solution.py:74
  131.5 3.1 fusion.31
  136.3 35.0 %reduce-scatter.11.cloned.1.call-done = f32[256,272]{0,1:T(8,128)} async-done(((f32[2048,272]{0,1:T(8,128)}), f32[256,272]{0,1:T(8,128)}) %reduce-scatter.11.cloned.1.call-update) | async-done | bytes 278544 | tf_op jit(solution)/shard_map/reduce_scatter | solution.py:77
  171.3 1.0 fusion.40
  172.3 9.9 %psum.65 = f32[256]{0:T(256)S(1)} all-reduce(f32[256]{0:T(256)S(1)} %get-tuple-element.68), channel_id=1, replica_groups=mesh['row'=4,'col'=8] {'row'}, use_global_device_ids=true, to_apply=%region_8.9 | all-reduce | flops 256 | bytes 2048 | tf_op jit(solution)/shard_map/psum | solution.py:33
  182.3 8.0 %psum.66 = f32[256]{0:T(256)S(1)} all-reduce(f32[256]{0:T(256)S(1)} %multiply_reduce_fusion.5), channel_id=1, replica_groups=mesh['row'=4,'col'=8] {'row'}, use_global_device_ids=true, to_apply=%region_10.11 | all-reduce | flops 256 | bytes 2048 | tf_op jit(solution)/shard_map/psum | solution.py:35
  192.0 4.4 all-gather.21.cloned.1.call-done
  196.4 4.7 fusion.21
  201.2 20.2 %all-gather.15.cloned.1.call-done = bf16[2048,272]{0,1:T(8,128)(2,1)} async-done(((bf16[256,272]{0,1:T(8,128)(2,1)}), bf16[2048,272]{0,1:T(8,128)(2,1)}) %all-gather.15.cloned.1.call-update) | async-done | bytes 1114128 | tf_op jit(solution)/shard_map/all_gather | solution.py:67
  221.4 2.3 copy.82
  223.7 3.5 all-to-all-start.1
  227.3 33.0 %all-gather.17.cloned.1.call-done = bf16[1088,544]{1,0:T(8,128)(2,1)} async-done(((bf16[272,544]{1,0:T(8,128)(2,1)}), bf16[1088,544]{1,0:T(8,128)(2,1)}) %all-gather.17.cloned.1.call-update) | async-done | bytes 1183760 | tf_op jit(solution)/shard_map/all_gather | solution.py:69
  260.3 57.9 %reduce-scatter.15.cloned.1.call-done = f32[512,544]{0,1:T(8,128)} async-done(((f32[2048,544]{0,1:T(8,128)}), f32[512,544]{0,1:T(8,128)}) %reduce-scatter.15.cloned.1.call-update) | async-done | bytes 1114128 | tf_op jit(solution)/shard_map/reduce_scatter | solution.py:105
  318.2 4.3 fusion.10
  322.5 2.5 fusion.45
  325.4 37.7 %all_to_all.48 = f32[4,512,272]{1,2,0:T(8,128)S(1)} all-to-all(f32[4,512,272]{1,2,0:T(8,128)S(1)} %pad_maximum_fusion), channel_id=1, replica_groups=mesh['row'=4,'col'=8] {'row'}, dimensions={0} | all-to-all | bytes 4456448 | tf_op jit(solution)/shard_map/all_to_all | solution.py:95
  363.1 1.6 copy.78
  364.9 7.5 %all-gather.19.cloned.1.call-done = bf16[2048,544]{0,1:T(8,128)(2,1)} async-done(((bf16[512,544]{0,1:T(8,128)(2,1)}), bf16[2048,544]{0,1:T(8,128)(2,1)}) %all-gather.19.cloned.1.call-update) | async-done | bytes 2228240 | tf_op jit(solution)/shard_map/all_gather | solution.py:74
  372.4 4.0 fusion.23
  376.5 34.6 %reduce-scatter.17.cloned.1.call-done = f32[256,272]{0,1:T(8,128)} async-done(((f32[2048,272]{0,1:T(8,128)}), f32[256,272]{0,1:T(8,128)}) %reduce-scatter.17.cloned.1.call-update) | async-done | bytes 278544 | tf_op jit(solution)/shard_map/reduce_scatter | solution.py:97
  411.1 1.2 multiply_reduce_fusion.1
  412.3 9.8 %all-reduce.2 = (f32[256]{0:T(256)S(1)}, f32[256]{0:T(256)S(1)}) all-reduce(f32[256]{0:T(256)S(1)} %get-tuple-element.53, f32[256]{0:T(256)S(1)} %get-tuple-element.54), channel_id=1, replica_groups=mesh['row'=4,'col'=8] {'row'}, use_global_device_ids=true, to_apply=%region_17.18 | all-reduce | flops 512 | bytes 4096 | tf_op jit(solution)/shard_map/psum | solution.py:47
  422.1 26.6 %reduce-scatter.13.cloned.1.call-done = f32[256,272]{0,1:T(8,128)} async-done(((f32[2048,272]{0,1:T(8,128)}), f32[256,272]{0,1:T(8,128)}) %reduce-scatter.13.cloned.1.call-update) | async-done | bytes 278544 | tf_op jit(solution)/shard_map/reduce_scatter | solution.py:77
  448.6 2.1 fusion.39
  450.8 23.0 %all-gather.23.cloned.1.call-done = bf16[2048,272]{0,1:T(8,128)(2,1)} async-done(((bf16[256,272]{0,1:T(8,128)(2,1)}), bf16[2048,272]{0,1:T(8,128)(2,1)}) %all-gather.23.cloned.1.call-update) | async-done | bytes 1114128 | tf_op jit(solution)/shard_map/all_gather | solution.py:101
  473.8 3.4 fusion.29
  477.3 3.8 fusion.43
  481.1 30.2 %reduce-scatter.19.cloned.1.call-done = f32[512,256]{1,0:T(8,128)} async-done(((f32[2048,256]{1,0:T(8,128)}), f32[512,256]{1,0:T(8,128)}) %reduce-scatter.19.cloned.1.call-update) | async-done | bytes 524304 | tf_op jit(solution)/shard_map/reduce_scatter | solution.py:105
  511.3 1.8 convert_element_type.82
  513.0 1.1 copy.63
  514.2 3.9 multiply_reduce_fusion
  518.1 1.3 multiply_convert_fusion
  520.6 1.3 convolution_bitcast_fusion
  522.0 1.3 copy-done.28
  523.3 1.0 fusion.46
  524.7 37.9 %all_to_all.49 = f32[4,512,272]{1,2,0:T(8,128)S(1)} all-to-all(f32[4,512,272]{1,2,0:T(8,128)S(1)} %pad_maximum_fusion.1), channel_id=1, replica_groups=mesh['row'=4,'col'=8] {'row'}, dimensions={0} | all-to-all | bytes 4456448 | tf_op jit(solution)/shard_map/all_to_all | solution.py:95
  562.7 1.6 copy.79
  564.5 2.8 fusion.41
  567.4 1.2 copy-done.13
  568.6 2.8 fusion.44
  571.4 1.4 fusion.20
  572.8 1.2 pad_maximum_fusion.4
  574.9 2.5 fusion.19
  577.4 1.2 pad_maximum_fusion.3
  581.8 28.9 %reduce-scatter.21.cloned.1.call-done = f32[256,272]{0,1:T(8,128)} async-done(((f32[2048,272]{0,1:T(8,128)}), f32[256,272]{0,1:T(8,128)}) %reduce-scatter.21.cloned.1.call-update) | async-done | bytes 278544 | tf_op jit(solution)/shard_map/reduce_scatter | solution.py:97
  610.7 1.2 multiply_reduce_fusion.2
  611.9 9.9 %all-reduce.1 = (f32[256]{0:T(256)S(1)}, f32[256]{0:T(256)S(1)}) all-reduce(f32[256]{0:T(256)S(1)} %get-tuple-element.51, f32[256]{0:T(256)S(1)} %get-tuple-element.55), channel_id=1, replica_groups=mesh['row'=4,'col'=8] {'row'}, use_global_device_ids=true, to_apply=%region_24.25 | all-reduce | flops 512 | bytes 4096 | tf_op jit(solution)/shard_map/psum | solution.py:47
  621.8 13.9 %psum.71 = f32[4,272]{1,0:T(4,128)S(1)} all-reduce(f32[4,272]{1,0:T(4,128)S(1)} %pad_maximum_fusion.7), channel_id=1, replica_groups=mesh['row'=4,'col'=8] {'col'}, use_global_device_ids=true, to_apply=%region_31.32 | all-reduce | flops 1088 | bytes 8704 | tf_op jit(solution)/shard_map/psum | solution.py:217
  637.0 1.8 multiply_add_fusion
  638.8 19.8 %reduce-scatter.23.cloned.1.call-done = f32[272,768]{1,0:T(8,128)} async-done(((f32[1088,768]{1,0:T(8,128)}), f32[272,768]{1,0:T(8,128)}) %reduce-scatter.23.cloned.1.call-update) | async-done | bytes 835600 | tf_op jit(solution)/shard_map/reduce_scatter | solution.py:88
  658.6 2.7 fusion.18
  661.3 1.3 pad_maximum_fusion.2
  (126 shorter events, 16.3 us)
Async XLA Ops:
  7.2 48.8 %all-gather.9.cloned.1.call-start = ((), (), s32[]{:S(2)}) async-start(), calls=%async_computation.12 | async-start | bytes 1253376 | tf_op jit(solution)/shard_map/all_gather | solution.py:67
  31.3 65.8 %all-gather.11.cloned.1.call-start = ((), (), s32[]{:S(2)}) async-start(), calls=%async_computation.13 | async-start | bytes 2088960 | tf_op jit(solution)/shard_map/all_gather | solution.py:69
  56.0 5.9 copy-start.27
  58.3 38.8 %all-to-all-start = ((bf16[4,512,272]{1,2,0:T(8,128)(2,1)}), bf16[4,512,272]{1,2,0:T(8,128)(2,1)S(1)}, u32[]{:S(2)}, u32[]{:S(2)}) async-start(bf16[4,512,272]{1,2,0:T(8,128)(2,1)} %bitcast.181), calls=%async_computation | async-start | bytes 2228224 | tf_op jit(solution)/shard_map/all_to_all | solution.py:68
  61.9 69.7 %all-gather.13.cloned.1.call-start = ((), (), s32[]{:S(2)}) async-start(), calls=%async_computation.14 | async-start | bytes 1310720 | tf_op jit(solution)/shard_map/all_gather | solution.py:74
  62.1 39.8 %copy-start.8 = (pred[512,512]{0,1:T(8,128)(4,1)}, pred[512,512]{0,1:T(8,128)(4,1)S(1)}, u32[]{:S(2)}) copy-start(pred[512,512]{0,1:T(8,128)(4,1)S(1)} %fusion.11) | copy-start | bytes 786436
  100.1 1.9 copy-start.11
  101.0 2.0 copy-start
  103.0 28.5 %copy-start.5 = (f32[256,272]{0,1:T(8,128)S(1)}, f32[256,272]{0,1:T(8,128)}, u32[]{:S(2)}) copy-start(f32[256,272]{0,1:T(8,128)} %param.16) | copy-start | bytes 835588
  105.0 66.3 %reduce-scatter.11.cloned.1.call-start = ((), (), s32[]{:S(2)}) async-start(), calls=%async_computation.15 | async-start | bytes 2506752 | tf_op jit(solution)/shard_map/reduce_scatter | solution.py:77
  134.6 1.0 copy-start.19
  134.6 36.7 %copy-start.2 = (f32[256,272]{0,1:T(8,128)S(1)}, f32[256,272]{0,1:T(8,128)}, u32[]{:S(2)}) copy-start(f32[256,272]{0,1:T(8,128)} %param.13) | copy-start | bytes 835588
  134.6 56.5 %copy-start.14 = (f32[272,544]{1,0:T(8,128)S(1)}, f32[272,544]{1,0:T(8,128)}, u32[]{:S(2)}) copy-start(f32[272,544]{1,0:T(8,128)} %param.17) | copy-start | bytes 1775620
  134.7 61.7 %copy-start.3 = (f32[544,272]{0,1:T(8,128)S(1)}, f32[544,272]{0,1:T(8,128)}, u32[]{:S(2)}) copy-start(f32[544,272]{0,1:T(8,128)} %param.18) | copy-start | bytes 1775620
  134.7 61.7 %all-gather.21.cloned.1.call-start = ((), (), s32[]{:S(2)}) async-start(), calls=%async_computation.20 | async-start | bytes 1253376 | tf_op jit(solution)/shard_map/all_gather | solution.py:101
  136.3 85.1 %all-gather.15.cloned.1.call-start = ((), (), s32[]{:S(2)}) async-start(), calls=%async_computation.16 | async-start | bytes 1253376 | tf_op jit(solution)/shard_map/all_gather | solution.py:67
  191.1 69.2 %all-gather.17.cloned.1.call-start = ((), (), s32[]{:S(2)}) async-start(), calls=%async_computation.17 | async-start | bytes 1740800 | tf_op jit(solution)/shard_map/all_gather | solution.py:69
  191.9 126.2 %reduce-scatter.15.cloned.1.call-start = ((), (), s32[]{:S(2)}) async-start(), calls=%async_computation.21 | async-start | bytes 5570560 | tf_op jit(solution)/shard_map/reduce_scatter | solution.py:105
  223.7 94.4 %all-to-all-start.1 = ((bf16[4,512,272]{1,2,0:T(8,128)(2,1)}), bf16[4,512,272]{1,2,0:T(8,128)(2,1)S(1)}, u32[]{:S(2)}, u32[]{:S(2)}) async-start(bf16[4,512,272]{1,2,0:T(8,128)(2,1)} %bitcast.190), calls=%async_computation.2 | async-start | bytes 2228224 | tf_op jit(solution)/shard_map/all_to_all | solution.py:68
  227.3 145.1 %all-gather.19.cloned.1.call-start = ((), (), s32[]{:S(2)}) async-start(), calls=%async_computation.18 | async-start | bytes 2785280 | tf_op jit(solution)/shard_map/all_gather | solution.py:74
  322.5 88.6 %reduce-scatter.17.cloned.1.call-start = ((), (), s32[]{:S(2)}) async-start(), calls=%async_computation.22 | async-start | bytes 2506752 | tf_op jit(solution)/shard_map/reduce_scatter | solution.py:97
  364.7 83.9 %reduce-scatter.13.cloned.1.call-start = ((), (), s32[]{:S(2)}) async-start(), calls=%async_computation.19 | async-start | bytes 2506752 | tf_op jit(solution)/shard_map/reduce_scatter | solution.py:77
  376.4 97.4 %all-gather.23.cloned.1.call-start = ((), (), s32[]{:S(2)}) async-start(), calls=%async_computation.23 | async-start | bytes 1253376 | tf_op jit(solution)/shard_map/all_gather | solution.py:101
  450.8 60.5 %reduce-scatter.19.cloned.1.call-start = ((), (), s32[]{:S(2)}) async-start(), calls=%async_computation.24 | async-start | bytes 2621440 | tf_op jit(solution)/shard_map/reduce_scatter | solution.py:105
  477.2 96.8 %reduce-scatter.25.cloned.1.call-start = ((), (), s32[]{:S(2)}) async-start(), calls=%async_computation.27 | async-start | bytes 3481600
  481.0 33.1 %copy-start.9 = (pred[512,512]{0,1:T(8,128)(4,1)S(1)}, pred[512,512]{0,1:T(8,128)(4,1)}, u32[]{:S(2)}) copy-start(pred[512,512]{0,1:T(8,128)(4,1)} %copy-done.8) | copy-start | bytes 786436
  481.0 33.1 %copy-start.12 = (bf16[512,768]{0,1:T(8,128)(2,1)S(1)}, bf16[512,768]{0,1:T(8,128)(2,1)}, u32[]{:S(2)}) copy-start(bf16[512,768]{0,1:T(8,128)(2,1)} %copy-done.11) | copy-start | bytes 2359300
  481.0 129.7 %reduce-scatter.21.cloned.1.call-start = ((), (), s32[]{:S(2)}) async-start(), calls=%async_computation.25 | async-start | bytes 2506752 | tf_op jit(solution)/shard_map/reduce_scatter | solution.py:97
  514.2 3.9 copy-start.1
  521.8 1.4 copy-start.28
  564.3 94.4 %reduce-scatter.23.cloned.1.call-start = ((), (), s32[]{:S(2)}) async-start(), calls=%async_computation.26 | async-start | bytes 4177920 | tf_op jit(solution)/shard_map/reduce_scatter | solution.py:88
  567.3 1.2 copy-start.13
  568.6 2.8 copy-start.17
  571.4 1.4 copy-start.22
  572.8 1.3 copy-start.15
  572.8 2.1 copy-start.18
  577.4 1.8 copy-start.4
  577.4 2.1 copy-start.7
  577.4 2.6 copy-start.6
  577.4 2.6 copy-start.23
  580.0 58.8 %copy-start.21 = (f32[256,272]{0,1:T(8,128)}, f32[256,272]{0,1:T(8,128)S(1)}, u32[]{:S(2)}) copy-start(f32[256,272]{0,1:T(8,128)S(1)} %fusion.42) | copy-start | bytes 835588
  580.0 55.7 %copy-start.24 = (f32[4,272]{1,0:T(4,128)S(1)}, f32[4,272]{1,0:T(4,128)}, u32[]{:S(2)}) copy-start(f32[4,272]{1,0:T(4,128)} %param.19) | copy-start | bytes 13060
  580.0 55.7 %copy-start.26 = (f32[2,4,272]{2,1,0:T(4,128)S(1)}, f32[2,4,272]{2,1,0:T(4,128)}, u32[]{:S(2)}) copy-start(f32[2,4,272]{2,1,0:T(4,128)} %param.24) | copy-start | bytes 26116
  580.0 57.0 %copy-start.20 = (f32[256,272]{0,1:T(8,128)S(1)}, f32[256,272]{0,1:T(8,128)}, u32[]{:S(2)}) copy-start(f32[256,272]{0,1:T(8,128)} %get-tuple-element.67) | copy-start | bytes 835588
  580.0 78.6 %copy-start.10 = (f32[272,768]{1,0:T(8,128)S(1)}, f32[272,768]{1,0:T(8,128)}, u32[]{:S(2)}) copy-start(f32[272,768]{1,0:T(8,128)} %param.15) | copy-start | bytes 2506756
  580.0 78.6 %copy-start.16 = (f32[2,272,768]{2,1,0:T(8,128)S(1)}, f32[2,272,768]{2,1,0:T(8,128)}, u32[]{:S(2)}) copy-start(f32[2,272,768]{2,1,0:T(8,128)} %param.20) | copy-start | bytes 5013508
  635.8 25.6 %copy-start.25 = (f32[4,272]{1,0:T(4,128)}, f32[4,272]{1,0:T(4,128)S(1)}, u32[]{:S(2)}) copy-start(f32[4,272]{1,0:T(4,128)S(1)} %psum.71) | copy-start | bytes 13060
Sparse Core Ops, SparseCore 0:
  31.4 24.5 all-gather.8
  58.4 38.7 all-gather.10
  105.1 26.3 all-gather.12
  134.8 36.4 reduce-scatter.10
  173.3 23.0 all-gather.20
  198.4 22.9 all-gather.14
  223.8 36.4 all-gather.16
  263.4 54.7 reduce-scatter.14
  322.6 49.7 all-gather.18
  374.5 36.4 reduce-scatter.16
  413.4 35.2 reduce-scatter.12
  450.9 22.8 all-gather.22
  477.3 33.8 reduce-scatter.18
  514.7 57.2 reduce-scatter.24
  574.2 36.4 reduce-scatter.20
  614.2 44.4 reduce-scatter.22
